TPU v7x, 32 devices: a whole 2x2x4 slice. The times are simulated.
32 devices in a mesh: blk: 8 (over y, x, core), rows: 4 (over z).
Axes of the slice: x: 2, y: 2, z: 4, core: 2. Of those that a mesh axis runs over, the one named last changes fastest.
Arguments:
- covariance: float32 [16384, 8, 8, 256], P('rows', None, 'blk'), may hold values from 0 to 5, as said below
- panel_order: int32 [64], replicated, may hold values from 0 to 63, each once
Outputs:
- factored: float32 [16384, 8, 8, 256], P('rows', None, 'blk')
Inputs may be any that keep to these rules, and one draw needn't show every extreme that they name: covariance is symmetric and positive definite. `panel_order`: every panel appears once; panel j is held by index j % 8 of blk.
All inputs are finite; a program needn't handle non-finite values.
Results may differ from a plain program's by a relative error of at most 0.0003.
Values sent between devices are 32-bit elements; how exact they have to be, the bound alone decides.
A program may use at most 192 MiB of HBM per device.

v0:
```python
import jax
import jax.numpy as jnp
from jax import lax
from jax.experimental import pallas as pl
from jax.experimental.pallas import tpu as pltpu
from jax.sharding import PartitionSpec as P

SECTIONS = 2
LANES = 128
HIGHEST = lax.Precision.HIGHEST


def split(values):
    high = values.astype(jnp.bfloat16)
    low = (values - high.astype(jnp.float32)).astype(jnp.bfloat16)
    return high, low


def update_kernel(keep_ref, old_ref, left_ref, right_ref, out_ref, right_parts):
    slots, depth, width = right_ref.shape
    rows = left_ref.shape[0]
    chunks = old_ref.shape[0] // rows
    halves = width // LANES

    @pl.when(pl.program_id(0) == 0)
    def _():
        for slot in range(slots):
            high, low = split(right_ref[slot])
            right_parts[slot, :depth, :] = high
            right_parts[slot, depth : 2 * depth, :] = low
            right_parts[slot, 2 * depth :, :] = high

    high, low = split(left_ref[...])
    left_parts = jnp.concatenate([high, high, low], axis=1)
    for slot in range(slots):
        change = jnp.dot(left_parts, right_parts[slot], preferred_element_type=jnp.float32)
        keep = keep_ref[slot] > 0
        for half in range(halves):
            at = pl.ds(slot * halves + half, rows, stride=chunks)
            out_ref[at, :] = jnp.where(keep, old_ref[at, :], 0.0) - change[:, half * LANES : (half + 1) * LANES]


def update(flat, keep, left, right):
    panels, rows, depth = left.shape
    slots, _, width = right.shape
    lines = flat.shape[0] // panels
    return pl.pallas_call(
        update_kernel,
        out_shape=jax.ShapeDtypeStruct(flat.shape, jnp.float32),
        grid_spec=pltpu.PrefetchScalarGridSpec(
            num_scalar_prefetch=1,
            grid=(panels,),
            in_specs=[
                pl.BlockSpec((lines, LANES), lambda i, keep: (i, 0)),
                pl.BlockSpec((None, rows, depth), lambda i, keep: (i, 0, 0)),
                pl.BlockSpec((slots, depth, width), lambda i, keep: (0, 0, 0)),
            ],
            out_specs=pl.BlockSpec((lines, LANES), lambda i, keep: (i, 0)),
            scratch_shapes=[pltpu.VMEM((slots, 3 * depth, width), jnp.bfloat16)],
        ),
        compiler_params=pltpu.CompilerParams(vmem_limit_bytes=56 << 20),
    )(keep, flat, left, right)


def local(covariance, panel_order):
    row_count, slots, _, width = covariance.shape
    owners = lax.axis_size("blk")
    row_blocks = lax.axis_size("rows")
    column_index = lax.axis_index("blk")
    row_index = lax.axis_index("rows")
    targets = [panel_order[section] for section in range(SECTIONS)]
    depth = SECTIONS * width
    row_panels = row_count // width
    view = covariance.reshape(row_count, slots, width)

    own = jnp.concatenate(
        [
            jnp.where(
                target % owners == column_index,
                lax.dynamic_index_in_dim(view, target // owners, 1, keepdims=False),
                0.0,
            )
            for target in targets
        ],
        axis=1,
    )
    block = jnp.concatenate(
        [
            jnp.where(
                target // row_panels == row_index,
                lax.dynamic_slice_in_dim(own, (target % row_panels) * width, width, 0),
                0.0,
            )
            for target in targets
        ],
        axis=0,
    )
    block = lax.psum(block, ("blk", "rows"))

    left = lax.psum(own, "blk").reshape(row_panels, width, depth)
    if row_panels % owners == 0:
        groups = row_panels // owners
        pieces = left.reshape(groups, owners, width, depth)
        mine = lax.dynamic_index_in_dim(pieces, column_index, 1, keepdims=False)
        across = lax.all_gather(mine, "rows", axis=0, tiled=True)
    else:
        across = jnp.concatenate(
            [
                jnp.where(
                    target // row_panels == row_index,
                    lax.dynamic_slice_in_dim(view, (target % row_panels) * width, width, 0),
                    0.0,
                )
                for target in targets
            ],
            axis=0,
        )
        across = lax.psum(across, "rows").transpose(1, 2, 0)

    lower = jnp.linalg.cholesky(block)
    inverse = lax.linalg.triangular_solve(
        lower, jnp.eye(depth, dtype=jnp.float32), left_side=True, lower=True
    )
    whole = jnp.dot(inverse.T, inverse, precision=HIGHEST)
    right = jnp.einsum("dk,pck->pdc", whole, across, precision=HIGHEST)
    slot_panels = jnp.arange(slots, dtype=jnp.int32) * owners + column_index
    keep = jnp.ones((slots,), jnp.int32)
    for section, target in enumerate(targets):
        here = slot_panels == target
        keep = jnp.where(here, 0, keep)
        solved = -inverse[section * width : (section + 1) * width].T
        right = jnp.where(here[:, None, None], solved[None], right)
    flat = covariance.reshape(row_count * slots * (width // LANES), LANES)
    return update(flat, keep, left, right).reshape(covariance.shape)


def solution(mesh):
    return jax.shard_map(
        local,
        mesh=mesh,
        in_specs=(P("rows", None, "blk", None), P()),
        out_specs=P("rows", None, "blk", None),
        check_vma=False,
    )
```

profile of v0, /device:TPU:0, one launch (start us, length us, event | category | flops | bytes accessed | tf_op | source)
XLA Modules:
  0.0 535.2 jit_solution(5080395423572216533)
XLA Ops:
  6.5 1.3 fusion.51
  13.0 8.5 %constant_dynamic-slice_fusion.3 = (f32[4096,1,1,256]{3,2,1,0:T(1,128)}, f32[4096,1,1,256]{3,2,1,0:T(1,128)}) fusion(f32[4096,8,1,256]{3,2,1,0:T(1,128)} %param.2, s32[]{:T(128)S(6)} %select_n.106, s32[]{:T(128)S(6)} %select_n.112), kind=kLoop, calls=%fused_computation.84 | loop fusion | bytes 16777224 | tf_op jit(solution)/shard_map/jit(dynamic_index_in_dim)/dynamic_slice | solution.py:80
  21.4 10.2 %copy.23 = f32[4096,1,1,256]{0,3,2,1:T(8,128)} copy(f32[4096,1,1,256]{3,2,1,0:T(1,128)} %get-tuple-element.26) | data formatting | bytes 8388608
  31.6 10.1 %copy.24 = f32[4096,1,1,256]{0,3,2,1:T(8,128)} copy(f32[4096,1,1,256]{3,2,1,0:T(1,128)} %get-tuple-element.27) | data formatting | bytes 8388608
  41.7 0.6 select_bitcast_fusion
  42.4 0.1 fusion.22
  42.5 1.8 copy-done
  44.3 1.3 copy-done.1
  45.6 1.2 pad_maximum_fusion.1
  46.9 7.9 %pad_maximum_fusion = f32[4096,512]{0,1:T(8,128)} fusion(f32[4096,256]{0,1:T(8,128)} %copy-done, f32[4096,256]{0,1:T(8,128)} %copy-done.1), kind=kLoop, calls=%fused_computation.4 | loop fusion | flops 2097152 | bytes 16777216 | tf_op jit(solution)/shard_map/concatenate | solution.py:76
  54.8 1.8 select_select_fusion.1
  56.6 0.1 iota_compare_fusion
  56.7 0.1 fusion.23
  56.8 125.7 %all-reduce.6.cloned.1.call-done = f32[512,512]{0,1:T(8,128)} async-done(((f32[512,512]{0,1:T(8,128)}), f32[512,512]{0,1:T(8,128)}) %all-reduce.6.cloned.1.call-update) | async-done | bytes 1048592 | tf_op jit(solution)/shard_map/psum | solution.py:98
  182.5 1.6 copy.15
  184.1 127.1 %all-reduce.4.cloned.1.call-done = f32[4096,512]{0,1:T(8,128)} async-done(((f32[4096,512]{0,1:T(8,128)}), f32[4096,512]{0,1:T(8,128)}) %all-reduce.4.cloned.1.call-update) | async-done | bytes 8388624 | tf_op jit(solution)/shard_map/psum | solution.py:100
  311.2 9.2 %copy.14 = f32[4096,512]{1,0:T(8,128)} copy(f32[4096,512]{0,1:T(8,128)} %all-reduce.4.cloned.1.call-done) | data formatting | bytes 16777216 | tf_op jit(solution)/shard_map/psum | solution.py:100
  320.3 2.4 constant_dynamic-slice_fusion.1
  322.7 0.2 fusion.12
  323.0 1.0 copy-done.3
  323.9 11.7 %cholesky.104 = f32[128,128]{1,0:T(8,128)S(1)} custom-call(f32[128,128]{1,0:T(8,128)S(1)} %cholesky.266), custom_call_target="Cholesky" | custom-call | tf_op jit(solution)/shard_map/jit(cholesky)/cholesky | solution.py:120
  335.7 9.8 %custom-call.30 = f32[1,128,128]{1,2,0:T(8,128)S(1)} custom-call(f32[1,128,128]{2,1,0:T(8,128)S(1)} %get-tuple-element.39), custom_call_target="InvertDiagBlocksLowerTriangular" | custom-call | tf_op jit(solution)/shard_map/jit(cholesky)/cholesky | solution.py:120
  345.5 0.1 cholesky.224
  345.6 1.2 constant_dynamic-update-slice_fusion
  346.9 1.3 convolution_subtract_fusion.3
  348.2 11.7 %cholesky.217 = f32[128,128]{1,0:T(8,128)S(1)} custom-call(f32[128,128]{1,0:T(8,128)S(1)} %cholesky.270), custom_call_target="Cholesky" | custom-call | tf_op jit(solution)/shard_map/jit(cholesky)/cholesky | solution.py:120
  359.9 10.0 %custom-call.31 = f32[1,128,128]{1,2,0:T(8,128)S(1)} custom-call(f32[1,128,128]{2,1,0:T(8,128)S(1)} %get-tuple-element.36), custom_call_target="InvertDiagBlocksLowerTriangular" | custom-call | tf_op jit(solution)/shard_map/jit(cholesky)/cholesky | solution.py:120
  369.9 0.3 convolution_dynamic-update-slice_fusion
  370.2 1.3 convolution_subtract_fusion.4
  371.5 11.7 %cholesky.238 = f32[128,128]{1,0:T(8,128)S(1)} custom-call(f32[128,128]{1,0:T(8,128)S(1)} %cholesky.275), custom_call_target="Cholesky" | custom-call | tf_op jit(solution)/shard_map/jit(cholesky)/cholesky | solution.py:120
  383.2 9.8 %custom-call.32 = f32[1,128,128]{1,2,0:T(8,128)S(1)} custom-call(f32[1,128,128]{2,1,0:T(8,128)S(1)} %get-tuple-element.33), custom_call_target="InvertDiagBlocksLowerTriangular" | custom-call | tf_op jit(solution)/shard_map/jit(cholesky)/cholesky | solution.py:120
  393.0 0.2 convolution_dynamic-update-slice_fusion.1
  393.3 1.2 convolution_subtract_fusion.5
  394.5 11.7 %cholesky.255 = f32[128,128]{1,0:T(8,128)S(1)} custom-call(f32[128,128]{1,0:T(8,128)S(1)} %convolution_subtract_fusion.5), custom_call_target="Cholesky" | custom-call | tf_op jit(solution)/shard_map/jit(cholesky)/cholesky | solution.py:120
  406.2 0.6 compare_reduce_fusion.3
  406.8 0.6 compare_reduce_fusion.2
  408.7 0.6 compare_reduce_fusion.1
  410.0 0.6 compare_reduce_fusion
  411.3 0.1 select_select_fusion
  411.5 10.1 %while.1 = (s32[]{:T(128)}, f32[512,512]{1,0:T(8,128)S(1)}, s32[4,2]{0,1:T(2,128)S(1)}, f32[4,128,128]{2,1,0:T(8,128)}, s32[]{:T(128)}) while((s32[]{:T(128)}, f32[512,512]{1,0:T(8,128)S(1)}, s32[4,2]{0,1:T(2,128)S(1)}, f32[4,128,128]{2,1,0:T(8,128)}, s32[]{:T(128)}) %tuple.32), condition=%wide.while_cond, body=%wide.while_body.sunk | while | flops 2 | bytes 132205 | solution.py:121
  411.5 0.1 constant_dynamic-slice_fusion.5
  411.5 0.5 fusion.59
  412.1 1.9 bitcast_dynamic-update-slice_fusion.2
  414.0 0.1 constant_dynamic-slice_fusion.5
  414.1 0.5 fusion.59
  414.6 1.9 bitcast_dynamic-update-slice_fusion.2
  416.5 0.1 constant_dynamic-slice_fusion.5
  416.6 0.5 fusion.59
  417.1 1.9 bitcast_dynamic-update-slice_fusion.2
  419.1 0.5 fusion.59
  419.6 1.9 bitcast_dynamic-update-slice_fusion.2
  421.6 40.5 %custom-call.33 = f32[4,128,128]{1,2,0:T(8,128)S(1)} custom-call(f32[4,128,128]{2,1,0:T(8,128)} %get-tuple-element.12), custom_call_target="InvertDiagBlocksLowerTriangular" | custom-call | tf_op jit(solution)/shard_map/triangular_solve | solution.py:121
  462.1 0.3 fusion.25
  462.4 0.4 convolution_subtract_fusion.1
  462.8 0.4 fusion.36
  463.2 0.4 convolution_subtract_fusion
  463.6 1.3 fusion.37
  464.9 0.6 convolution_subtract_fusion.2
  465.6 1.3 fusion.34
  466.9 0.2 copy.16
  467.1 0.2 copy.17
  467.3 2.8 convolution_bitcast_fusion
  470.2 10.2 %fusion.right_ref = f32[8,512,256]{2,1,0:T(8,128)} fusion(f32[512,256]{1,0:T(8,128)S(1)} %copy.17, f32[512,256]{1,0:T(8,128)S(1)} %copy.16, pred[8]{0:T(512)(128)(4,1)S(1)} %get-tuple-element.22, pred[8]{0:T(512)(128)(4,1)S(1)} %get-tuple-element.23, f32[512,512,1]{1,0,2:T(8,128)} %convolution_bitcast_fusion, f32[8,1,256,512]{3,2,1,0:T(8,128)} %all-gather.3.cloned.1.call-done), kind=kOutput, calls=%fused_computation.8 | convolution fusion | flops 6444548096 | bytes 10485776 | tf_op jit(solution)/shard_map/dk,pck->pdc/dot_general | solution.py:125
  480.4 48.1 %shard_map.28 = f32[65536,128]{1,0:T(8,128)} custom-call(s32[8]{0:T(128)} %get-tuple-element.21.keep_ref, f32[65536,128]{1,0:T(8,128)} %bitcast.74, f32[16,256,512]{2,1,0:T(8,128)} %bitcast.76, f32[8,512,256]{2,1,0:T(8,128)} %fusion.right_ref), custom_call_target="tpu_custom_call" | custom-call | tf_op jit(solution)/shard_map/pallas_call | solution.py:47
  (27 shorter events, 0.5 us)
Async XLA Ops:
  6.5 176.0 %all-reduce.6.cloned.1.call-start = ((), (), s32[]{:S(2)}) async-start(), calls=%async_computation.1 | async-start | bytes 2097152 | tf_op jit(solution)/shard_map/psum | solution.py:98
  42.4 1.9 copy-start
  42.4 3.2 copy-start.1
  46.8 264.4 %all-reduce.4.cloned.1.call-start = ((), (), s32[]{:S(2)}) async-start(), calls=%async_computation | async-start | bytes 16777216 | tf_op jit(solution)/shard_map/psum | solution.py:100
  54.8 415.4 %all-gather.3.cloned.1.call-start = ((), (), s32[]{:S(2)}) async-start(), calls=%async_computation.2 | async-start | bytes 5242880 | tf_op jit(solution)/shard_map/all_gather | solution.py:105
  184.1 138.6 %copy-start.2 = (f32[512,512]{0,1:T(8,128)S(1)}, f32[512,512]{0,1:T(8,128)}, u32[]{:S(2)}) copy-start(f32[512,512]{0,1:T(8,128)} %all-reduce.6.cloned.1.call-done) | copy-start | bytes 3145732
  323.0 1.0 copy-start.3
  462.1 0.7 copy-start.4
Sparse Core Ops, SparseCore 0:
  46.9 135.5 all-reduce.5
  186.0 125.1 all-reduce.3
  322.8 80.8 all-gather.2
where the time goes:
time: 539 us; the launch traced here: 535 us
  waiting for transfers between devices  253 us (47%)
  other arithmetic  132 us (24%)
  local copies, waits for them, and re-layouts  57.8 us (11%)
  Pallas kernels  48.1 us (9%)
  matrix products  23.2 us (4%)
  between operations  21.2 us (4%)
    psum x1, waiting for transfers between devices, local(): left = lax.psum(own, 'blk').reshape(row_panels, width, depth)  127 us
    psum x1, waiting for transfers between devices, local(): block = lax.psum(block, ('blk', 'rows'))  126 us
    another operation x15, other arithmetic, local(): lower = jnp.linalg.cholesky(block)  79.2 us
    pallas_call x1, Pallas kernels, update(): pl.pallas_call(update_kernel, out_shape=jax.ShapeDtypeStruct(flat.shape,...  48.1 us
    another operation x3, other arithmetic, local(): lax.linalg.triangular_solve(lower, jnp.eye(depth, dtype=jnp.float32), lef...  40.6 us
    unnamed x12, local copies, waits for them, and re-layouts  24.3 us
  transfers between devices with their start and end apart: 3, of which 2 were waited for; matrix products, arithmetic and copies ran while one was open for 29% of the time, Pallas kernels for 0%

commit v1 on v0

v1 whole, which is shorter than its diff:
```python
import functools

import jax
import jax.numpy as jnp
from jax import lax
from jax.experimental import pallas as pl
from jax.experimental.pallas import tpu as pltpu
from jax.sharding import PartitionSpec as P

SECTIONS = 2
LANES = 128
CHUNKS = 8
TILE = 128
MESH = pl.DeviceIdType.MESH
HIGHEST = lax.Precision.HIGHEST


def split(values):
    high = values.astype(jnp.bfloat16)
    low = (values - high.astype(jnp.float32)).astype(jnp.bfloat16)
    return high, low


def exchange_kernel(
    row_blocks, owners, chunks, root_ref, side_ref, own_ref, across_ref, left_ref,
    from_low, from_high, to_high, to_low, send_high, send_low, recv_low, recv_high,
    send_chip, recv_chip, send_pair, recv_pair,
):
    z = lax.axis_index("rows")
    me = lax.axis_index("blk")
    last = row_blocks - 1
    chips = owners // 2
    chip, core = me // 2, me % 2
    pair = chip * 2 + 1 - core
    rows = own_ref.shape[0] // chunks
    span = left_ref.shape[2]
    columns = pl.ds(pl.multiple_of(z * span, LANES), span)
    reach = jnp.maximum(z, last - z)

    def lines(c):
        return pl.ds(pl.multiple_of(c * rows, 8), rows)

    def mate(d):
        return (chip + d) % chips * 2 + core

    def source(d):
        return (chip + chips - d) % chips * 2 + core

    def along(src, dst, send, recv, c, step):
        return pltpu.make_async_remote_copy(
            src_ref=src.at[lines(c)], dst_ref=dst.at[lines(c)], send_sem=send.at[c], recv_sem=recv.at[c],
            device_id={"rows": z + step}, device_id_type=MESH,
        )

    def to_mate(d, c):
        return pltpu.make_async_remote_copy(
            src_ref=across_ref.at[lines(c), columns], dst_ref=left_ref.at[me, lines(c)],
            send_sem=send_chip.at[d - 1, c], recv_sem=recv_chip.at[d - 1, c],
            device_id={"blk": mate(d)}, device_id_type=MESH,
        )

    def to_pair(d, c):
        who = source(d)
        src = across_ref.at[lines(c), columns] if d == 0 else left_ref.at[who, lines(c)]
        return pltpu.make_async_remote_copy(
            src_ref=src, dst_ref=left_ref.at[who, lines(c)],
            send_sem=send_pair.at[d, c], recv_sem=recv_pair.at[d, c],
            device_id={"blk": pair}, device_id_type=MESH,
        )

    barrier = pltpu.get_barrier_semaphore()
    for d in range(1, chips):
        pl.semaphore_signal(barrier, inc=1, device_id={"blk": mate(d)}, device_id_type=MESH)
    pl.semaphore_signal(barrier, inc=1, device_id={"blk": pair}, device_id_type=MESH)

    @pl.when(z > 0)
    def _():
        pl.semaphore_signal(barrier, inc=1, device_id={"rows": z - 1}, device_id_type=MESH)

    @pl.when(z < last)
    def _():
        pl.semaphore_signal(barrier, inc=1, device_id={"rows": z + 1}, device_id_type=MESH)

    ends = jnp.where(z > 0, 1, 0) + jnp.where(z < last, 1, 0)
    pl.semaphore_wait(barrier, chips + ends)

    def valid(c):
        return jnp.logical_and(c >= 0, c < chunks)

    def step(t, carry):
        c = t - z

        @pl.when(valid(c))
        def _():
            @pl.when(z == 0)
            def _():
                along(own_ref, from_low, send_high, recv_low, c, 1).start()

            @pl.when(z > 0)
            def _():
                along(to_high, from_low, send_high, recv_low, c, 0).wait_recv()

            @pl.when(jnp.logical_and(z > 0, z < last))
            def _():
                here = root_ref[c] > 0
                to_high[lines(c), :] = jnp.where(here, own_ref[lines(c), :], from_low[lines(c), :])
                along(to_high, from_low, send_high, recv_low, c, 1).start()

        e = t - (last - z)

        @pl.when(valid(e))
        def _():
            @pl.when(z == last)
            def _():
                along(own_ref, from_high, send_low, recv_high, e, -1).start()

            @pl.when(z < last)
            def _():
                along(to_low, from_high, send_low, recv_high, e, 0).wait_recv()

            @pl.when(jnp.logical_and(z > 0, z < last))
            def _():
                here = root_ref[e] > 0
                to_low[lines(e), :] = jnp.where(here, own_ref[lines(e), :], from_high[lines(e), :])
                along(to_low, from_high, send_low, recv_high, e, -1).start()

        f = t - reach

        @pl.when(valid(f))
        def _():
            here = root_ref[f] > 0
            above = side_ref[f] > 0

            @pl.when(z == 0)
            def _():
                across_ref[lines(f), :] = jnp.where(here, own_ref[lines(f), :], from_high[lines(f), :])

            @pl.when(z == last)
            def _():
                across_ref[lines(f), :] = jnp.where(here, own_ref[lines(f), :], from_low[lines(f), :])

            @pl.when(jnp.logical_and(z > 0, z < last))
            def _():
                far = jnp.where(above, from_low[lines(f), :], from_high[lines(f), :])
                across_ref[lines(f), :] = jnp.where(here, own_ref[lines(f), :], far)

            left_ref[me, lines(f), :] = across_ref[lines(f), columns]
            for d in range(1, chips):
                to_mate(d, f).start()
            to_pair(0, f).start()

        g = f - 1

        @pl.when(valid(g))
        def _():
            for d in range(1, chips):
                to_mate(d, g).wait_recv()
                to_pair(d, g).start()

        return carry

    lax.fori_loop(0, chunks + last + 1, step, 0)

    def finish(c, carry):
        @pl.when(z < last)
        def _():
            along(own_ref, from_low, send_high, recv_low, c, 1).wait_send()

        @pl.when(z > 0)
        def _():
            along(own_ref, from_high, send_low, recv_high, c, -1).wait_send()

        for d in range(1, chips):
            to_mate(d, c).wait_send()
        for d in range(chips):
            to_pair(d, c).wait_send()
            to_pair(d, c).wait_recv()
        return carry

    lax.fori_loop(0, chunks, finish, 0)


def exchange(own, root, side, row_blocks, owners):
    depth, total = own.shape
    span = total // row_blocks
    chips = owners // 2
    flow = pltpu.VMEM((depth, total), jnp.float32)
    dma = pltpu.SemaphoreType.DMA
    line = [dma((CHUNKS,))] * 4
    memory = pl.BlockSpec(memory_space=pltpu.VMEM)
    scalars = pl.BlockSpec(memory_space=pltpu.SMEM)
    return pl.pallas_call(
        functools.partial(exchange_kernel, row_blocks, owners, CHUNKS),
        out_shape=(
            jax.ShapeDtypeStruct((depth, total), jnp.float32),
            jax.ShapeDtypeStruct((owners, depth, span), jnp.float32),
        ),
        in_specs=[scalars, scalars, memory],
        out_specs=(memory, memory),
        scratch_shapes=[flow] * 4 + line
        + [dma((chips - 1, CHUNKS))] * 2 + [dma((chips, CHUNKS))] * 2,
        compiler_params=pltpu.CompilerParams(
            collective_id=0, has_side_effects=True, vmem_limit_bytes=56 << 20
        ),
        cost_estimate=pl.CostEstimate(flops=0, bytes_accessed=400_000_000, transcendentals=0),
    )(root, side, own)


def product(a, b, dims):
    return lax.dot_general(a, b, (dims, ((), ())), precision=HIGHEST, preferred_element_type=jnp.float32)


def invert_tile(tile):
    size = tile.shape[0]
    row_of = lax.broadcasted_iota(jnp.int32, (size, size), 0)
    column_of = lax.broadcasted_iota(jnp.int32, (size, size), 1)
    right = jnp.where(row_of == column_of, 1.0, 0.0).astype(jnp.float32)
    sub = 8
    left_rows = [tile[i : i + sub] for i in range(0, size, sub)]
    right_rows = [right[i : i + sub] for i in range(0, size, sub)]
    index = lax.broadcasted_iota(jnp.int32, (sub, size), 0)
    scales = [jnp.zeros((sub, size), jnp.float32) for _ in left_rows]
    for k in range(size):
        at, inner = divmod(k, sub)
        pivot = jnp.broadcast_to(left_rows[at][inner : inner + 1, k : k + 1], (1, size))
        scale = 1.0 / pivot
        left_row = left_rows[at][inner : inner + 1, :] * scale
        right_row = right_rows[at][inner : inner + 1, :] * scale
        scales[at] = jnp.where(index == inner, lax.rsqrt(pivot), scales[at])
        for i in range(at, len(left_rows)):
            column = jnp.broadcast_to(left_rows[i][:, k : k + 1], (sub, size))
            if i == at:
                column = jnp.where(index > inner, column, 0.0)
            left_rows[i] = left_rows[i] - column * left_row
            right_rows[i] = right_rows[i] - column * right_row
    return jnp.concatenate([r * s for r, s in zip(right_rows, scales)], axis=0)


def factor_kernel(block_ref, inverse_ref, whole_ref, work, lower, tiles):
    size = block_ref.shape[0]
    count = size // TILE
    work[...] = block_ref[...]
    inverse_ref[...] = jnp.zeros_like(inverse_ref)

    def one(i, carry):
        at = pl.ds(pl.multiple_of(i * TILE, TILE), TILE)
        tile = invert_tile(work[at, at])
        tiles[i] = tile
        below = product(work[:, at], tile, ((1,), (1,)))
        row_of = lax.broadcasted_iota(jnp.int32, below.shape, 0)
        below = jnp.where(row_of >= (i + 1) * TILE, below, 0.0)
        lower[:, at] = below
        work[...] -= product(below, below, ((1,), (1,)))
        return carry

    lax.fori_loop(0, count, one, 0)
    for i in range(count):
        at = slice(i * TILE, (i + 1) * TILE)
        inverse_ref[at, at] = tiles[i]
        if i:
            done = slice(0, i * TILE)
            seen = product(lower[at, done], inverse_ref[done, done], ((1,), (0,)))
            inverse_ref[at, done] = -product(tiles[i], seen, ((1,), (0,)))
    inverse = inverse_ref[...]
    whole_ref[...] = product(inverse, inverse, ((0,), (0,)))


def factor(block):
    size = block.shape[0]
    square = jax.ShapeDtypeStruct((size, size), jnp.float32)
    return pl.pallas_call(
        factor_kernel,
        out_shape=(square, square),
        scratch_shapes=[
            pltpu.VMEM((size, size), jnp.float32),
            pltpu.VMEM((size, size), jnp.float32),
            pltpu.VMEM((size // TILE, TILE, TILE), jnp.float32),
        ],
        compiler_params=pltpu.CompilerParams(vmem_limit_bytes=32 << 20),
    )(block)


def update_kernel(keep_ref, old_ref, left_ref, right_ref, out_ref, right_parts):
    slots = keep_ref.shape[0]
    depth, rows = left_ref.shape
    width = right_ref.shape[1] // slots
    chunks = old_ref.shape[0] // rows
    halves = width // LANES

    @pl.when(pl.program_id(0) == 0)
    def _():
        for slot in range(slots):
            at = slice(slot * width, (slot + 1) * width)
            high, low = split(right_ref[:, at])
            right_parts[slot, :depth, :] = high
            right_parts[slot, depth : 2 * depth, :] = low
            right_parts[slot, 2 * depth :, :] = high

    high, low = split(left_ref[...].T)
    left_parts = jnp.concatenate([high, high, low], axis=1)
    for slot in range(slots):
        change = jnp.dot(left_parts, right_parts[slot], preferred_element_type=jnp.float32)
        keep = keep_ref[slot] > 0
        for half in range(halves):
            at = pl.ds(slot * halves + half, rows, stride=chunks)
            out_ref[at, :] = jnp.where(keep, old_ref[at, :], 0.0) - change[:, half * LANES : (half + 1) * LANES]


def update(flat, keep, left, right, width):
    groups, depth, span = left.shape
    slots = keep.shape[0]
    panels = groups * span // width
    lines = flat.shape[0] // panels
    return pl.pallas_call(
        update_kernel,
        out_shape=jax.ShapeDtypeStruct(flat.shape, jnp.float32),
        grid_spec=pltpu.PrefetchScalarGridSpec(
            num_scalar_prefetch=1,
            grid=(panels,),
            in_specs=[
                pl.BlockSpec((lines, LANES), lambda i, keep: (i, 0)),
                pl.BlockSpec((None, depth, width), lambda i, keep: (lax.rem(i, groups), 0, lax.div(i, groups))),
                pl.BlockSpec(right.shape, lambda i, keep: (0, 0)),
            ],
            out_specs=pl.BlockSpec((lines, LANES), lambda i, keep: (i, 0)),
            scratch_shapes=[pltpu.VMEM((slots, 3 * depth, width), jnp.bfloat16)],
        ),
        compiler_params=pltpu.CompilerParams(vmem_limit_bytes=56 << 20),
    )(keep, flat, left, right)


def local(covariance, panel_order):
    row_count, slots, _, width = covariance.shape
    owners = lax.axis_size("blk")
    row_blocks = lax.axis_size("rows")
    column_index = lax.axis_index("blk")
    row_index = lax.axis_index("rows")
    targets = [panel_order[section] for section in range(SECTIONS)]
    depth = SECTIONS * width
    row_panels = row_count // width
    roots = [target // row_panels for target in targets]

    strips = [
        lax.dynamic_slice_in_dim(covariance, (target % row_panels) * width, width, 0).reshape(width, slots * width)
        for target in targets
    ]
    own = jnp.concatenate(strips, axis=0)
    block = jnp.concatenate(
        [
            jnp.where(
                target % owners == column_index,
                lax.dynamic_slice_in_dim(own, (target // owners) * width, width, 1),
                0.0,
            )
            for target in targets
        ],
        axis=1,
    )
    here = jnp.repeat(jnp.stack(roots) == row_index, width)
    block = lax.psum(lax.psum(jnp.where(here[:, None], block, 0.0), "blk"), "rows")

    if row_panels % owners == 0 and owners % 2 == 0 and row_blocks > 1 and CHUNKS % SECTIONS == 0:
        share = CHUNKS // SECTIONS
        root = jnp.repeat(jnp.stack(roots) == row_index, share).astype(jnp.int32)
        side = jnp.repeat(jnp.stack(roots) < row_index, share).astype(jnp.int32)
        across, left = exchange(own, root, side, row_blocks, owners)
    else:
        across = lax.psum(jnp.where(here[:, None], own, 0.0), "rows")
        panels = jnp.concatenate(
            [
                jnp.where(
                    target % owners == column_index,
                    lax.dynamic_index_in_dim(covariance, target // owners, 1, keepdims=False)[:, 0],
                    0.0,
                )
                for target in targets
            ],
            axis=1,
        )
        left = lax.psum(panels, "blk").reshape(row_panels, width, depth).transpose(0, 2, 1)

    inverse, whole = factor(block)
    right = jnp.dot(whole, across, precision=HIGHEST).reshape(depth, slots, width)
    slot_panels = jnp.arange(slots, dtype=jnp.int32) * owners + column_index
    keep = jnp.ones((slots,), jnp.int32)
    for section, target in enumerate(targets):
        match = slot_panels == target
        keep = jnp.where(match, 0, keep)
        solved = -inverse[section * width : (section + 1) * width].T
        right = jnp.where(match[None, :, None], solved[:, None, :], right)
    flat = covariance.reshape(row_count * slots * (width // LANES), LANES)
    return update(flat, keep, left, right.reshape(depth, slots * width), width).reshape(covariance.shape)


def solution(mesh):
    return jax.shard_map(
        local,
        mesh=mesh,
        in_specs=(P("rows", None, "blk", None), P()),
        out_specs=P("rows", None, "blk", None),
        check_vma=False,
    )
```

time: 539 us -> 392 us (0.73)
  Pallas kernels: 48.1 us -> 267 us
  waiting for transfers between devices: 253 us -> 59.6 us
  other arithmetic: 132 us -> 4.4 us
  local copies, waits for them, and re-layouts: 57.8 us -> 32.5 us
  matrix products: 23.2 us -> 8.82 us
    pallas_call x0 -> x2, Pallas kernels: none -> 217 us  [the longest x1 165 us: exchange(): pl.pallas_call(functools.partial(exchange_kernel, row_blocks, owners, CHU...]
    psum x2, waiting for transfers between devices: 253 us -> 59.5 us  [the longest x1 59.5 us: local(): lax.psum(jnp.where(here[:, None], block, 0.0), 'blk')]
    another operation x18 -> x0, other arithmetic: 120 us -> none  [the longest x15 79.2 us: local(): lower = jnp.linalg.cholesky(block)]
    unnamed x12 -> x11, local copies, waits for them, and re-layouts: 24.3 us -> 12.5 us
    psum x2 -> x0, local copies, waits for them, and re-layouts: 10.7 us -> none  [the longest x1 9.15 us: local(): left = lax.psum(own, 'blk').reshape(row_panels, width, depth)]
    another operation x17 -> x0, local copies, waits for them, and re-layouts: 10.2 us -> none
    another operation x13 -> x0, matrix products: 10.2 us -> none  [the longest x6 5.47 us: local(): lower = jnp.linalg.cholesky(block)]
    concatenate x2 -> x0, other arithmetic: 9.05 us -> none  [the longest x1 7.86 us: local(): jnp.concatenate([jnp.where(target % owners == column_index, lax.dynamic_i...]
  transfers between devices with their start and end apart: 3 -> 2, of which waited for: 2 -> 1; matrix products, arithmetic and copies ran while one was open for 29% -> 1% of each run, Pallas kernels for 0% -> 42%
where the time goes in v1:
time: 392 us; the launch traced here: 391 us
  Pallas kernels  267 us (68%)
  waiting for transfers between devices  59.6 us (15%)
  local copies, waits for them, and re-layouts  32.5 us (8%)
  between operations  18.6 us (5%)
  matrix products  8.82 us (2%)
  other arithmetic  4.4 us (1%)
    pallas_call x1, Pallas kernels, exchange(): pl.pallas_call(functools.partial(exchange_kernel, row_blocks, owners, CHU...  165 us
    psum x1, waiting for transfers between devices, local(): lax.psum(jnp.where(here[:, None], block, 0.0), 'blk')  59.5 us
    pallas_call x1, Pallas kernels, factor(): pl.pallas_call(factor_kernel, out_shape=(square, square), scratch_shapes=...  52.8 us
    pallas_call x1, Pallas kernels, update(): pl.pallas_call(update_kernel, out_shape=jax.ShapeDtypeStruct(flat.shape,...  49.2 us
    dynamic_slice x1, local copies, waits for them, and re-layouts, local(): lax.dynamic_slice_in_dim(covariance, target % row_panels * width, width, 0)  14.6 us
    unnamed x11, local copies, waits for them, and re-layouts  12.5 us
    dot_general x1, matrix products, local(): jnp.dot(whole, across, precision=HIGHEST).reshape(depth, slots, width)  8.82 us
  transfers between devices with their start and end apart: 2, of which 1 were waited for; matrix products, arithmetic and copies ran while one was open for 1% of the time, Pallas kernels for 42%

profile of v1, /device:TPU:0, one launch (start us, length us, event | category | flops | bytes accessed | tf_op | source)
XLA Modules:
  0.0 390.6 jit_solution(315837322092622604)
XLA Ops:
  6.5 0.0 all-reduce.3.cloned.1.call-start
  6.5 1.3 fusion.5
  12.9 0.1 fusion.2
  13.0 0.1 broadcast_in_dim.81
  13.1 14.6 %dynamic-slice_reduce_fusion = (f32[256,8,256]{2,1,0:T(8,128)}, f32[256,8,256]{2,1,0:T(8,128)S(1)}) fusion(f32[4096,8,1,256]{3,2,1,0:T(1,128)} %param.2, s32[]{:T(128)S(6)} %select_n.85, s32[]{:T(128)S(6)} %select_n.83), kind=kLoop, calls=%fused_computation.1 | loop fusion | bytes 8388616 | tf_op jit(solution)/shard_map/dynamic_slice | solution.py:344
  27.7 4.0 %copy.7 = f32[32,8,8,256]{3,1,2,0:T(8,128)} copy(f32[32,8,8,256]{3,2,1,0:T(8,128)} %bitcast.26) | data formatting | bytes 4194304
  31.6 0.9 copy.6
  32.5 0.0 copy-start.1
  32.5 1.5 constant_dynamic-update-slice_fusion.1
  34.0 0.9 copy-done.1
  34.9 1.5 constant_dynamic-update-slice_fusion.own_ref
  36.3 1.3 dynamic-slice_select_fusion.1
  37.6 1.1 maximum_select_fusion
  38.7 0.0 all-reduce.3.cloned.1.call-update
  38.8 0.0 all-reduce.5.cloned.1.call-start
  38.8 59.5 %all-reduce.3.cloned.1.call-done = f32[512,512]{1,0:T(8,128)} async-done(((f32[512,512]{1,0:T(8,128)}), f32[512,512]{1,0:T(8,128)}) %all-reduce.3.cloned.1.call-update) | async-done | bytes 1048592 | tf_op jit(solution)/shard_map/psum | solution.py:360
  98.3 0.0 all-reduce.5.cloned.1.call-update
  98.3 0.1 broadcast_in_dim.76
  98.4 0.6 convert_element_type.11.root_ref
  99.1 0.1 broadcast_in_dim.77
  99.1 0.6 convert_element_type.13.side_ref
  99.8 1.8 select_select_fusion.1
  101.6 0.1 broadcast_in_dim.88
  101.7 0.1 broadcast_in_dim.78
  101.8 164.7 %shard_map.28 = (f32[512,2048]{1,0:T(8,128)}, f32[8,512,512]{2,1,0:T(8,128)}) custom-call(s32[8]{0:T(128)} %convert_element_type.11.root_ref, s32[8]{0:T(128)} %convert_element_type.13.side_ref, f32[512,2048]{1,0:T(8,128)} %constant_dynamic-update-slice_fusion.own_ref), custom_call_target="tpu_custom_call" | custom-call | bytes 400000000 | tf_op jit(solution)/shard_map/pallas_call | solution.py:192
  266.5 0.0 all-reduce.5.cloned.1.call-done.block_ref
  266.5 0.0 copy-start
  266.5 1.2 copy-done
  267.7 52.8 %shard_map.29 = (f32[512,512]{1,0:T(8,128)S(1)}, f32[512,512]{1,0:T(8,128)S(1)}) custom-call(f32[512,512]{1,0:T(8,128)S(1)} %copy-done), custom_call_target="tpu_custom_call" | custom-call | tf_op jit(solution)/shard_map/pallas_call | solution.py:271
  320.5 0.1 negate_bitcast_fusion
  320.6 0.2 copy.4
  320.8 0.2 copy.3
  321.0 0.3 broadcast_in_dim.86
  321.3 2.0 copy.8
  323.3 0.3 broadcast_in_dim.91
  323.6 0.0 copy-start.2
  323.6 2.0 copy.9
  325.6 0.2 copy-done.2
  325.8 8.8 %select_select_fusion.right_ref = f32[512,2048]{1,0:T(8,128)} fusion(f32[512,2048]{1,0:T(8,128)S(1)} %bitcast.21, f32[512,2048]{1,0:T(8,128)S(1)} %bitcast.22, f32[512,512]{1,0:T(8,128)S(1)} %get-tuple-element.11, f32[512,2048]{1,0:T(8,128)S(1)} %copy-done.2, pred[2048]{0:T(1024)(128)(4,1)S(1)} %broadcast_in_dim.89, pred[2048]{0:T(1024)(128)(4,1)S(1)} %broadcast_in_dim.79), kind=kOutput, calls=%fused_computation | convolution fusion | flops 6444548096 | bytes 17829888 | tf_op jit(solution)/shard_map/dot_general | solution.py:383
  334.6 49.2 %shard_map.30 = f32[65536,128]{1,0:T(8,128)} custom-call(s32[8]{0:T(128)} %get-tuple-element.17.keep_ref, f32[65536,128]{1,0:T(8,128)} %bitcast.20, f32[8,512,512]{2,1,0:T(8,128)} %get-tuple-element.9.left_ref, f32[512,2048]{1,0:T(8,128)} %select_select_fusion.right_ref), custom_call_target="tpu_custom_call" | custom-call | tf_op jit(solution)/shard_map/pallas_call | solution.py:314
  (3 shorter events, 0.0 us)
Async XLA Ops:
  6.5 91.8 %all-reduce.3.cloned.1.call-start = ((), (), s32[]{:S(2)}) async-start(), calls=%async_computation | async-start | bytes 2097152 | tf_op jit(solution)/shard_map/psum | solution.py:360
  32.5 2.3 copy-start.1
  38.8 227.7 %all-reduce.5.cloned.1.call-start = ((), (), s32[]{:S(2)}) async-start(), calls=%async_computation.1 | async-start | bytes 2097152 | tf_op jit(solution)/shard_map/psum | solution.py:360
  266.5 1.2 copy-start
  323.6 2.2 copy-start.2
Sparse Core Ops, SparseCore 0:
  38.9 59.4 all-reduce.2
  100.7 81.8 all-reduce.4

commit v2 on v1

--- a/solution.py
+++ b/solution.py
@@ -357,7 +357,7 @@
         axis=1,
     )
     here = jnp.repeat(jnp.stack(roots) == row_index, width)
-    block = lax.psum(lax.psum(jnp.where(here[:, None], block, 0.0), "blk"), "rows")
+    block = lax.psum(jnp.where(here[:, None], block, 0.0), ("blk", "rows"))
 
     if row_panels % owners == 0 and owners % 2 == 0 and row_blocks > 1 and CHUNKS % SECTIONS == 0:
         share = CHUNKS // SECTIONS

time: 392 us -> 317 us (0.81)
  waiting for transfers between devices: 59.6 us -> 0.04 us
  Pallas kernels: 267 us -> 252 us
    psum x2 -> x1, waiting for transfers between devices: 59.5 us -> 0.02 us  [local(): block = lax.psum(jnp.where(here[:, None], block, 0.0), ('blk', 'rows'))]
    pallas_call x1, Pallas kernels: 165 us -> 150 us  [exchange(): pl.pallas_call(functools.partial(exchange_kernel, row_blocks, owners, CHU...]
  transfers between devices with their start and end apart: 2 -> 1, of which waited for: 1 -> 0; matrix products, arithmetic and copies ran while one was open for 1% -> 1% of each run, Pallas kernels for 42% -> 47%
where the time goes in v2:
time: 317 us
  Pallas kernels  252 us (79%)
  local copies, waits for them, and re-layouts  32.5 us (10%)
  between operations  18.6 us (6%)
  matrix products  8.82 us (3%)
  other arithmetic  4.41 us (1%)
    pallas_call x1, Pallas kernels, exchange(): pl.pallas_call(functools.partial(exchange_kernel, row_blocks, owners, CHU...  150 us
    pallas_call x1, Pallas kernels, factor(): pl.pallas_call(factor_kernel, out_shape=(square, square), scratch_shapes=...  52.8 us
    pallas_call x1, Pallas kernels, update(): pl.pallas_call(update_kernel, out_shape=jax.ShapeDtypeStruct(flat.shape,...  49.2 us
    dynamic_slice x1, local copies, waits for them, and re-layouts, local(): lax.dynamic_slice_in_dim(covariance, target % row_panels * width, width, 0)  14.6 us
    unnamed x11, local copies, waits for them, and re-layouts  12.5 us
    dot_general x1, matrix products, local(): jnp.dot(whole, across, precision=HIGHEST).reshape(depth, slots, width)  8.82 us
  transfers between devices with their start and end apart: 1, of which 0 were waited for; matrix products, arithmetic and copies ran while one was open for 1% of the time, Pallas kernels for 47%

profile of v2, /device:TPU:0, one launch (start us, length us, event | category | flops | bytes accessed | tf_op | source)
XLA Modules:
  0.0 316.5 jit_solution(3323285564704441962)
XLA Ops:
  6.5 0.0 all-reduce.2.cloned.1.call-start
  6.5 1.3 fusion.5
  12.9 0.1 fusion.2
  13.0 0.1 broadcast_in_dim.81
  13.1 14.6 %dynamic-slice_reduce_fusion = (f32[256,8,256]{2,1,0:T(8,128)}, f32[256,8,256]{2,1,0:T(8,128)S(1)}) fusion(f32[4096,8,1,256]{3,2,1,0:T(1,128)} %param.2, s32[]{:T(128)S(6)} %select_n.85, s32[]{:T(128)S(6)} %select_n.83), kind=kLoop, calls=%fused_computation.1 | loop fusion | bytes 8388616 | tf_op jit(solution)/shard_map/dynamic_slice | solution.py:344
  27.7 4.0 %copy.7 = f32[32,8,8,256]{3,1,2,0:T(8,128)} copy(f32[32,8,8,256]{3,2,1,0:T(8,128)} %bitcast.26) | data formatting | bytes 4194304
  31.6 0.9 copy.6
  32.5 0.0 copy-start.1
  32.5 1.5 constant_dynamic-update-slice_fusion.1
  34.0 0.9 copy-done.1
  34.9 1.5 constant_dynamic-update-slice_fusion.own_ref
  36.3 1.3 dynamic-slice_select_fusion.1
  37.6 1.1 maximum_select_fusion
  38.7 0.0 all-reduce.2.cloned.1.call-update
  38.8 0.1 broadcast_in_dim.76
  38.8 0.6 convert_element_type.11.root_ref
  39.5 0.1 broadcast_in_dim.77
  39.5 0.6 convert_element_type.13.side_ref
  40.2 1.8 select_select_fusion.1
  42.0 0.1 broadcast_in_dim.88
  42.1 0.1 broadcast_in_dim.78
  42.2 150.2 %shard_map.28 = (f32[512,2048]{1,0:T(8,128)}, f32[8,512,512]{2,1,0:T(8,128)}) custom-call(s32[8]{0:T(128)} %convert_element_type.11.root_ref, s32[8]{0:T(128)} %convert_element_type.13.side_ref, f32[512,2048]{1,0:T(8,128)} %constant_dynamic-update-slice_fusion.own_ref), custom_call_target="tpu_custom_call" | custom-call | bytes 400000000 | tf_op jit(solution)/shard_map/pallas_call | solution.py:192
  192.4 0.0 all-reduce.2.cloned.1.call-done.block_ref
  192.4 0.0 copy-start
  192.4 1.2 copy-done
  193.6 52.8 %shard_map.29 = (f32[512,512]{1,0:T(8,128)S(1)}, f32[512,512]{1,0:T(8,128)S(1)}) custom-call(f32[512,512]{1,0:T(8,128)S(1)} %copy-done), custom_call_target="tpu_custom_call" | custom-call | tf_op jit(solution)/shard_map/pallas_call | solution.py:271
  246.4 0.1 negate_bitcast_fusion
  246.6 0.2 copy.4
  246.8 0.2 copy.3
  247.0 0.3 broadcast_in_dim.86
  247.3 2.0 copy.8
  249.2 0.3 broadcast_in_dim.91
  249.5 0.0 copy-start.2
  249.5 2.0 copy.9
  251.5 0.2 copy-done.2
  251.7 8.8 %select_select_fusion.right_ref = f32[512,2048]{1,0:T(8,128)} fusion(f32[512,2048]{1,0:T(8,128)S(1)} %bitcast.21, f32[512,2048]{1,0:T(8,128)S(1)} %bitcast.22, f32[512,512]{1,0:T(8,128)S(1)} %get-tuple-element.11, f32[512,2048]{1,0:T(8,128)S(1)} %copy-done.2, pred[2048]{0:T(1024)(128)(4,1)S(1)} %broadcast_in_dim.89, pred[2048]{0:T(1024)(128)(4,1)S(1)} %broadcast_in_dim.79), kind=kOutput, calls=%fused_computation | convolution fusion | flops 6444548096 | bytes 17829888 | tf_op jit(solution)/shard_map/dot_general | solution.py:383
  260.5 49.2 %shard_map.30 = f32[65536,128]{1,0:T(8,128)} custom-call(s32[8]{0:T(128)} %get-tuple-element.17.keep_ref, f32[65536,128]{1,0:T(8,128)} %bitcast.20, f32[8,512,512]{2,1,0:T(8,128)} %get-tuple-element.9.left_ref, f32[512,2048]{1,0:T(8,128)} %select_select_fusion.right_ref), custom_call_target="tpu_custom_call" | custom-call | tf_op jit(solution)/shard_map/pallas_call | solution.py:314
  (3 shorter events, 0.0 us)
Async XLA Ops:
  6.5 185.9 %all-reduce.2.cloned.1.call-start = ((), (), s32[]{:S(2)}) async-start(), calls=%async_computation | async-start | bytes 2097152 | tf_op jit(solution)/shard_map/psum | solution.py:360
  32.5 2.3 copy-start.1
  192.4 1.2 copy-start
  249.5 2.2 copy-start.2
Sparse Core Ops, SparseCore 0:
  38.9 136.3 all-reduce.1
